TPU v7x, 128 devices: a whole 4x4x4 slice. The times are simulated.
128 devices in a mesh: leaf: 128 (over y, z, x, core).
Axes of the slice: x: 4, y: 4, z: 4, core: 2. Of those that a mesh axis runs over, the one named last changes fastest.
Arguments:
- density: bfloat16 [131072, 220], P('leaf'), may hold values from -6 to 6
- vel_mask: int32 [131072], P('leaf'), may hold values from 0 to 1, as said below
- near_list: int32 [131072, 27], P('leaf'), may hold values from 0 to 131071, as said below
- near_ops: bfloat16 [27, 220, 660], replicated, may hold values from -0.078125 to 0.078125
- upward_ops: bfloat16 [8, 220, 56], replicated, may hold values from -0.0068359375 to 0.0068359375
- coupling_operators: float32 [56, 168], replicated, may hold values from -0.75 to 0.75
- coarse_weights: float32 [32, 32], replicated, may hold values from -1 to 1
- downward_ops: bfloat16 [8, 56, 220], replicated, may hold values from -0.75 to 0.75
- conc_owner: int32 [131072, 1], P('leaf'), may hold values from 0 to 127; in each aligned block of 1024 rows (0 to 1023, 1024 to 2047, ...) at most 16 rows name the same one
- concentration: bfloat16 [262144, 220], P('leaf'), may hold values from -6 to 6
- departure: int32 [262144], P('leaf'), may hold values from 0 to 2047
- departure_class: int32 [262144], P('leaf'), may hold values from 0 to 7
- shift_ops: bfloat16 [8, 220, 220], replicated, may hold values from -0.4375 to 0.4375
- eval_ops: bfloat16 [220, 1024], replicated, may hold values from -0.4375 to 0.4375
Outputs:
- velocity: bfloat16 [131072, 660], P('leaf')
- advected: bfloat16 [262144, 256], P('leaf')
Inputs may be any that keep to these rules, and one draw needn't show every extreme that they name: `vel_mask`: in each aligned block of 1024 rows the real leaves come first; every block has from 341 to 1024 real leaves, and both counts occur in every draw. `near_list`: entry [i, t] lies within 1024 of i; column 13 is i itself. `conc_owner`: in each aligned block of 1024 rows, the rows of one device, no owner is named more than 16 times, a bound that some block reaches. `departure`: A slot index within the same device's 2048 slots.
All inputs are finite; a program needn't handle non-finite values.
Results may differ from a plain program's by a relative error of at most 0.008.
Values may be sent and summed in bfloat16 or wider, within the bound.
No kernel may reach another device: no remote copies, remote signals or barrier semaphores. Data moves between devices by JAX's collectives and lax.ppermute only.
A program may use at most 128 MiB of HBM per device.

v0:
```python
import jax
import jax.numpy as jnp
from jax import lax
from jax.sharding import PartitionSpec as P

SPAN = 4
time_step = 0.5


def with_halo(block, sides, width):
    for axis, dim in sides:
        count = lax.axis_size(axis)
        forward = [(i, i + 1) for i in range(count - 1)]
        backward = [(target, source) for source, target in forward]
        low = lax.ppermute(
            lax.slice_in_dim(block, block.shape[dim] - width, None, axis=dim), axis, forward
        )
        high = lax.ppermute(lax.slice_in_dim(block, 0, width, axis=dim), axis, backward)
        block = jnp.concatenate([low, block, high], axis=dim)
    return block


def shifted_rows(gathered, classes, shift_ops):
    kinds = shift_ops.shape[0]
    total = jnp.zeros((gathered.shape[0], shift_ops.shape[2]), jnp.float32)
    for kind in range(kinds):
        product = jnp.dot(gathered, shift_ops[kind], preferred_element_type=jnp.float32)
        total = jnp.where((classes == kind)[:, None], product, total)
    return total.astype(jnp.bfloat16)


def advect_rows(base, velocity_rows, alive_rows, eval_ops):
    value_rows = jnp.dot(base, eval_ops, preferred_element_type=jnp.float32)
    nodes_count = value_rows.shape[1] // 4
    speeds = jnp.dot(
        velocity_rows.reshape(-1, eval_ops.shape[0]),
        eval_ops[:, :nodes_count],
        preferred_element_type=jnp.float32,
    )
    speeds = speeds.reshape(base.shape[0], 3, nodes_count)
    correction = speeds[:, 0] * value_rows[:, nodes_count : 2 * nodes_count]
    correction = correction + speeds[:, 1] * value_rows[:, 2 * nodes_count : 3 * nodes_count]
    correction = correction + speeds[:, 2] * value_rows[:, 3 * nodes_count :]
    return (alive_rows[:, None] * (value_rows[:, :nodes_count] - time_step * correction)).astype(
        jnp.bfloat16
    )


def local(
    density,
    vel_mask,
    near_list,
    near_ops,
    upward_ops,
    coupling_operators,
    coarse_weights,
    downward_ops,
    conc_owner,
    concentration,
    departure,
    departure_class,
    shift_ops,
    eval_ops,
):
    leaves = density.shape[0]
    coef_width = density.shape[1]
    devices = lax.axis_size("leaf")
    my_index = lax.axis_index("leaf")
    alive = vel_mask.astype(jnp.float32)
    live_density = (density.astype(jnp.float32) * alive[:, None]).astype(jnp.bfloat16)
    padded = with_halo(live_density, (("leaf", 0),), leaves)
    local_rows = near_list - my_index * leaves + leaves

    def near_step(position, total):
        rows = lax.dynamic_index_in_dim(local_rows, position, 1, keepdims=False)
        picked = jnp.take(padded, rows, axis=0)
        operator = lax.dynamic_index_in_dim(near_ops, position, 0, keepdims=False)
        return total + jnp.dot(picked, operator, preferred_element_type=jnp.float32)

    nearby_field = lax.fori_loop(
        0, near_ops.shape[0], near_step, jnp.zeros((leaves, 3 * coef_width), jnp.float32)
    )
    parts = jnp.einsum(
        "gop,opq->goq",
        live_density.reshape(-1, 8, coef_width),
        upward_ops,
        preferred_element_type=jnp.float32,
    )
    own_part = jnp.sum(parts, axis=(0, 1))
    boxes = devices // SPAN
    my_box = my_index // SPAN
    box_rows = (jnp.arange(boxes, dtype=jnp.int32) == my_box).astype(jnp.float32)
    moments = lax.psum(box_rows[:, None] * own_part[None, :], "leaf")
    expanded = jnp.dot(moments, coupling_operators, precision=lax.Precision.HIGHEST)
    weight_row = lax.dynamic_slice_in_dim(coarse_weights, my_box, 1, 0)
    own_expansion = jnp.dot(weight_row, expanded, precision=lax.Precision.HIGHEST)
    box_far = jnp.einsum(
        "jq,oqp->ojp",
        own_expansion.reshape(3, -1),
        downward_ops.astype(jnp.float32),
        precision=lax.Precision.HIGHEST,
    )
    far_field = jnp.broadcast_to(
        box_far.reshape(1, 8, 3 * coef_width), (leaves // 8, 8, 3 * coef_width)
    ).reshape(leaves, 3 * coef_width)
    velocity = ((nearby_field + far_field) * alive[:, None]).astype(jnp.bfloat16)
    slots_here = concentration.shape[0]
    capacity = slots_here // devices
    owner = conc_owner[:, 0]
    onehot = (owner[:, None] == jnp.arange(devices, dtype=jnp.int32)[None, :]).astype(jnp.int32)
    rank = jnp.sum(jnp.cumsum(onehot, axis=0) * onehot, axis=1) - 1
    send_slot = owner * capacity + rank
    placement = (jnp.arange(slots_here, dtype=jnp.int32)[:, None] == send_slot[None, :]).astype(
        jnp.bfloat16
    )
    send_velocity = jnp.dot(placement, velocity, preferred_element_type=jnp.float32).astype(
        jnp.bfloat16
    )
    send_alive = jnp.dot(
        placement, vel_mask.astype(jnp.bfloat16), preferred_element_type=jnp.float32
    ).astype(jnp.bfloat16)
    got_velocity, got_alive = (
        lax.all_to_all(
            send_velocity.reshape(devices, capacity, -1),
            "leaf",
            split_axis=0,
            concat_axis=0,
            tiled=True,
        ),
        lax.all_to_all(
            send_alive.reshape(devices, capacity), "leaf", split_axis=0, concat_axis=0, tiled=True
        ),
    )
    base = shifted_rows(concentration[departure], departure_class, shift_ops)
    advected = advect_rows(
        base,
        got_velocity.reshape(slots_here, -1),
        got_alive.reshape(slots_here).astype(jnp.float32),
        eval_ops,
    )
    return (velocity, advected)


def solution(mesh):
    placed = (
        P("leaf", None),
        P("leaf"),
        P("leaf", None),
        P(),
        P(),
        P(),
        P(),
        P(),
        P("leaf", None),
        P("leaf", None),
        P("leaf"),
        P("leaf"),
        P(),
        P(),
    )
    return jax.shard_map(
        local,
        mesh=mesh,
        in_specs=placed,
        out_specs=(P("leaf", None), P("leaf", None)),
        check_vma=False,
    )
```

profile of v0, /device:TPU:1, one launch (start us, length us, event | category | flops | bytes accessed | tf_op | source)
XLA Modules:
  0.0 428.8 jit_solution(9726396116737616334)
XLA Ops:
  13.9 14.0 %all-to-all-start = ((bf16[128,1,16]{2,1,0:T(2,128)(2,1)}), bf16[128,1,16]{2,1,0:T(2,128)(2,1)S(1)}, u32[]{:S(2)}, u32[]{:S(2)}) async-start(bf16[128,1,16]{2,1,0:T(2,128)(2,1)} %all_to_all.12), calls=%async_computation | async-start | bytes 131072 | tf_op jit(solution)/shard_map/all_to_all | solution.py:130
  28.7 67.2 %psum.7 = f32[32,56]{1,0:T(8,128)S(1)} all-reduce(f32[32,56]{1,0:T(8,128)S(1)} %broadcast_multiply_fusion), channel_id=1, replica_groups=mesh['leaf'=128] {'leaf'}, use_global_device_ids=true, to_apply=%region_3.4 | all-reduce | flops 1792 | bytes 14336 | tf_op jit(solution)/shard_map/psum | solution.py:93
  99.5 7.5 %gather_fusion.1 = bf16[2048,220]{1,0:T(8,128)(2,1)S(1)} fusion(bf16[2048,220]{1,0:T(8,128)(2,1)S(1)} %copy.42, s32[2048]{0:T(1024)S(1)} %fusion.46), kind=kCustom, calls=%fused_computation.1 | custom fusion | bytes 1810432 | tf_op jit(solution)/shard_map/gather | solution.py:134
  111.1 237.2 %while.14 = (s32[]{:T(128)}, f32[1024,660]{0,1:T(8,128)}, s32[1024,27]{0,1:T(8,128)}, bf16[3072,220]{1,0:T(8,128)(2,1)S(1)}, bf16[27,220,660]{1,2,0:T(8,128)(2,1)}, /*index=5*/s32[]{:T(128)}, s32[]{:T(128)}) while((s32[]{:T(128)}, f32[1024,660]{0,1:T(8,128)}, s32[1024,27]{0,1:T(8,128)}, bf16[3072,220]{1,0:T(8,128)(2,1)S(1)}, ...), condition=%wide.region_1.2_spmd.clone, body=%wide.region_0.1_spmd.clone.sunk | while | flops 298953728 | bytes 7137383 | solution.py:80
  123.7 4.1 select_add_fusion.2
  141.4 4.1 select_add_fusion.2
  150.2 4.1 select_add_fusion.2
  159.0 4.1 select_add_fusion.2
  167.8 4.1 select_add_fusion.2
  176.6 4.1 select_add_fusion.2
  185.4 4.1 select_add_fusion.2
  194.3 4.1 select_add_fusion.2
  203.1 4.1 select_add_fusion.2
  211.9 4.1 select_add_fusion.2
  220.7 4.1 select_add_fusion.2
  229.5 4.1 select_add_fusion.2
  238.3 4.1 select_add_fusion.2
  247.2 4.1 select_add_fusion.2
  256.0 4.1 select_add_fusion.2
  264.8 4.1 select_add_fusion.2
  273.6 4.1 select_add_fusion.2
  282.4 4.1 select_add_fusion.2
  300.1 4.1 select_add_fusion.2
  317.7 4.1 select_add_fusion.2
  335.3 4.1 select_add_fusion.2
  353.9 4.5 %fusion.11 = bf16[2048,660]{0,1:T(8,128)(2,1)} fusion(bf16[1024,660]{1,0:T(8,128)(2,1)S(1)} %fusion.13, s32[1024]{0:T(1024)S(1)} %add_add_fusion), kind=kOutput, calls=%fused_computation.18 | convolution fusion | flops 2771689472 | bytes 4059136 | tf_op jit(solution)/shard_map/dot_general | solution.py:116
  358.3 4.6 %copy.51 = bf16[2048,660]{1,0:T(8,128)(2,1)} copy(bf16[2048,660]{0,1:T(8,128)(2,1)} %fusion.11) | data formatting | bytes 5406720 | tf_op jit(solution)/shard_map/convert_element_type | solution.py:116
  363.0 5.7 %all-to-all-start.1 = ((bf16[128,16,660]{2,1,0:T(8,128)(2,1)}), bf16[128,16,660]{2,1,0:T(8,128)(2,1)}, u32[]{:S(2)}, u32[]{:S(2)}) async-start(bf16[128,16,660]{2,1,0:T(8,128)(2,1)} %bitcast.102), calls=%async_computation.1 | async-start | bytes 6291456 | tf_op jit(solution)/shard_map/all_to_all | solution.py:123
  374.9 6.4 %fusion.28 = f32[2048,1024]{1,0:T(8,128)} fusion(bf16[220,1024]{1,0:T(8,128)(2,1)S(1)} %copy-done.4, bf16[2048,220]{0,1:T(8,128)(2,1)} %fusion.41, bf16[2048,220]{0,1:T(8,128)(2,1)} %fusion.19, bf16[2048,220]{1,0:T(8,128)(2,1)S(1)} %gather_fusion.1, pred[2048]{0:T(1024)(128)(4,1)S(1)} %get-tuple-element.144, pred[2048]{0:T(1024)(128)(4,1)S(1)} %get-tuple-element.139, ...), kind=kOutput, calls=%fused_computation.46 | convolution fusion | flops 1121894400 | bytes 11643424 | tf_op jit(solution)/shard_map/dot_general | solution.py:33
  383.1 27.0 %all-to-all-done.1 = bf16[128,16,660]{2,1,0:T(8,128)(2,1)} async-done(((bf16[128,16,660]{2,1,0:T(8,128)(2,1)}), bf16[128,16,660]{2,1,0:T(8,128)(2,1)}, u32[]{:S(2)}, u32[]{:S(2)}) %all-to-all-start.1) | async-done | bytes 2703392 | tf_op jit(solution)/shard_map/all_to_all | solution.py:123
  410.1 10.8 %dot_general.78 = bf16[2048,3,220]{2,1,0:T(4,128)(2,1)} reshape(bf16[128,16,660]{2,1,0:T(8,128)(2,1)} %all-to-all-done.1) | data formatting | bytes 5406720 | tf_op jit(solution)/shard_map/dot_general | solution.py:35
  424.1 4.6 %fusion.26 = bf16[2048,256]{1,0:T(8,128)(2,1)} fusion(f32[2048,1024]{1,0:T(8,128)} %fusion.28, f32[2048,3,256]{2,0,1:T(8,128)S(1)} %fusion.14, f32[2048]{0:T(1024)S(1)} %reshape.89), kind=kLoop, calls=%fused_computation.38 | loop fusion | flops 4718592 | bytes 15736832 | tf_op jit(solution)/shard_map/convert_element_type | solution.py:44
  (171 shorter events, 189.5 us)
Async XLA Ops:
  0.6 96.4 %copy-start = (bf16[8,56,220]{2,1,0:T(8,128)(2,1)S(1)}, bf16[8,56,220]{2,1,0:T(8,128)(2,1)}, u32[]{:S(2)}) copy-start(bf16[8,56,220]{2,1,0:T(8,128)(2,1)} %param.23) | copy-start | bytes 591364
  0.6 10.6 %copy-start.13 = (s32[1024,1]{0,1:T(1,128)S(1)}, s32[1024,1]{0,1:T(1,128)}, u32[]{:S(2)}) copy-start(s32[1024,1]{0,1:T(1,128)} %param.24) | copy-start | bytes 12292
  3.6 105.8 %collective-permute-start.1 = (bf16[1024,220]{1,0:T(8,128)(2,1)}, bf16[1024,220]{1,0:T(8,128)(2,1)}, u32[]{:S(2)}, u32[]{:S(2)}) collective-permute-start(bf16[1024,220]{1,0:T(8,128)(2,1)} %multiply_convert_fusion), channel_id=1, source_target_pairs={{1,0},{2,1},{3,2},{4,3},{5,4},{6,5},{7,6},{8,7},{9,8},{10,9},{11,1... | collective-permute-start | bytes 1351688 | tf_op jit(solution)/shard_map/ppermute | solution.py:18
  6.9 102.5 %collective-permute-start = (bf16[1024,220]{1,0:T(8,128)(2,1)}, bf16[1024,220]{1,0:T(8,128)(2,1)}, u32[]{:S(2)}, u32[]{:S(2)}) collective-permute-start(bf16[1024,220]{1,0:T(8,128)(2,1)} %multiply_convert_fusion), channel_id=1, source_target_pairs={{0,1},{1,2},{2,3},{3,4},{4,5},{5,6},{6,7},{7,8},{8,9},{9,10},{10,1... | collective-permute-start | bytes 1351688 | tf_op jit(solution)/shard_map/ppermute | solution.py:15
  11.3 16.9 %copy-start.15 = (s32[2048]{0:T(1024)S(1)}, s32[2048]{0:T(1024)}, u32[]{:S(2)}) copy-start(s32[2048]{0:T(1024)} %param.26) | copy-start | bytes 24580
  11.3 16.9 %copy-start.14 = (s32[2048]{0:T(1024)S(1)}, s32[2048]{0:T(1024)}, u32[]{:S(2)}) copy-start(s32[2048]{0:T(1024)} %param.27) | copy-start | bytes 24580
  11.3 16.9 %copy-start.16 = (bf16[8,220,56]{1,2,0:T(8,128)(2,1)S(1)}, bf16[8,220,56]{1,2,0:T(8,128)(2,1)}, u32[]{:S(2)}) copy-start(bf16[8,220,56]{1,2,0:T(8,128)(2,1)} %param.20) | copy-start | bytes 591364
  11.7 84.2 %copy-start.12 = (f32[56,168]{1,0:T(8,128)S(1)}, f32[56,168]{1,0:T(8,128)}, u32[]{:S(2)}) copy-start(f32[56,168]{1,0:T(8,128)} %param.21) | copy-start | bytes 112900
  11.7 85.7 %copy-start.3 = (bf16[2048,220]{0,1:T(8,128)(2,1)S(1)}, bf16[2048,220]{0,1:T(8,128)(2,1)}, u32[]{:S(2)}) copy-start(bf16[2048,220]{0,1:T(8,128)(2,1)} %param.25) | copy-start | bytes 2703364
  13.9 349.1 %all-to-all-start = ((bf16[128,1,16]{2,1,0:T(2,128)(2,1)}), bf16[128,1,16]{2,1,0:T(2,128)(2,1)S(1)}, u32[]{:S(2)}, u32[]{:S(2)}) async-start(bf16[128,1,16]{2,1,0:T(2,128)(2,1)} %all_to_all.12), calls=%async_computation | async-start | bytes 131072 | tf_op jit(solution)/shard_map/all_to_all | solution.py:130
  99.5 7.5 %copy-start.2 = (bf16[8,220,220]{2,0,1:T(8,128)(2,1)S(1)}, bf16[8,220,220]{2,0,1:T(8,128)(2,1)}, u32[]{:S(2)}) copy-start(bf16[8,220,220]{2,0,1:T(8,128)(2,1)} %param.28) | copy-start | bytes 2323204
  363.0 5.7 %copy-start.9 = (bf16[1,220,220]{2,0,1:T(2,128)(2,1)S(1)}, bf16[1,220,220]{2,0,1:T(2,128)(2,1)}, u32[]{:S(2)}) copy-start(bf16[1,220,220]{2,0,1:T(2,128)(2,1)} %get-tuple-element.132) | copy-start | bytes 290404
  363.0 6.2 %copy-start.8 = (bf16[1,220,220]{2,0,1:T(2,128)(2,1)S(1)}, bf16[1,220,220]{2,0,1:T(2,128)(2,1)}, u32[]{:S(2)}) copy-start(bf16[1,220,220]{2,0,1:T(2,128)(2,1)} %get-tuple-element.133) | copy-start | bytes 290404
  363.0 47.1 %all-to-all-start.1 = ((bf16[128,16,660]{2,1,0:T(8,128)(2,1)}), bf16[128,16,660]{2,1,0:T(8,128)(2,1)}, u32[]{:S(2)}, u32[]{:S(2)}) async-start(bf16[128,16,660]{2,1,0:T(8,128)(2,1)} %bitcast.102), calls=%async_computation.1 | async-start | bytes 6291456 | tf_op jit(solution)/shard_map/all_to_all | solution.py:123
  368.6 1.1 copy-start.7
  368.7 1.6 copy-start.6
  369.2 1.6 copy-start.5
  369.8 2.5 copy-start.11
  372.3 0.9 copy-start.10
  372.9 2.0 copy-start.4
  424.1 4.6 %copy-start.1 = (bf16[8,56,220]{2,1,0:T(8,128)(2,1)S(1)}, bf16[8,56,220]{2,1,0:T(8,128)(2,1)}, u32[]{:S(2)}) copy-start(bf16[8,56,220]{2,1,0:T(8,128)(2,1)} %param.23) | copy-start | bytes 591364
where the time goes:
time: 432 us; the launch traced here: 429 us
  local copies, waits for them, and re-layouts  141 us (33%)
  matrix products  132 us (31%)
  blocking collectives  67.2 us (16%)
  other arithmetic  34.3 us (8%)
  waiting for transfers between devices  27 us (6%)
  starting transfers between devices  26.1 us (6%)
    dot_general x27, matrix products, near_step(): return total + jnp.dot(picked, operator, preferred_element_type=jnp.float32)  109 us
    gather x27, local copies, waits for them, and re-layouts, near_step(): picked = jnp.take(padded, rows, axis=0)  106 us
    psum x1, blocking collectives, local(): moments = lax.psum(box_rows[:, None] * own_part[None, :], 'leaf')  67.2 us
    all_to_all x1, waiting for transfers between devices, local(): lax.all_to_all(send_velocity.reshape(devices, capacity, -1), 'leaf', spli...  27 us
    and x27, other arithmetic, near_step(): picked = jnp.take(padded, rows, axis=0)  21.3 us
    all_to_all x1, starting transfers between devices, local(): lax.all_to_all(send_alive.reshape(devices, capacity), 'leaf', split_axis=...  14 us
    dot_general x1, local copies, waits for them, and re-layouts, advect_rows(): jnp.dot(velocity_rows.reshape(-1, eval_ops.shape[0]), eval_ops[:, :nodes_...  10.8 us
  transfers between devices with their start and end apart: 4, of which 1 were waited for; matrix products, arithmetic and copies ran while one was open for 66% of the time, Pallas kernels for 0%

commit v1 on v0

--- a/solution.py
+++ b/solution.py
@@ -1,3 +1,4 @@
+import functools
 import jax
 import jax.numpy as jnp
 from jax import lax
@@ -5,6 +6,14 @@
 
 SPAN = 4
 time_step = 0.5
+
+
+def _supply_ways(local_block, net_axis):
+    local_out = jnp.sum(lax.all_gather(local_block, net_axis), axis=0)
+    return local_out
+
+
+_draw_steps_all = functools.partial(_supply_ways, net_axis="leaf")
 
 
 def with_halo(block, sides, width):
@@ -90,7 +99,7 @@
     boxes = devices // SPAN
     my_box = my_index // SPAN
     box_rows = (jnp.arange(boxes, dtype=jnp.int32) == my_box).astype(jnp.float32)
-    moments = lax.psum(box_rows[:, None] * own_part[None, :], "leaf")
+    moments = _draw_steps_all(box_rows[:, None] * own_part[None, :])
     expanded = jnp.dot(moments, coupling_operators, precision=lax.Precision.HIGHEST)
     weight_row = lax.dynamic_slice_in_dim(coarse_weights, my_box, 1, 0)
     own_expansion = jnp.dot(weight_row, expanded, precision=lax.Precision.HIGHEST)

time: 432 us -> 409 us (0.947)
  blocking collectives: 67.2 us -> 41.8 us
    psum x1 -> x0, blocking collectives: 67.2 us -> none  [local(): moments = lax.psum(box_rows[:, None] * own_part[None, :], 'leaf')]
    all_gather x0 -> x1, blocking collectives: none -> 41.8 us  [_supply_ways(): local_out = jnp.sum(lax.all_gather(local_block, net_axis), axis=0)]
  transfers between devices with their start and end apart: 4 -> 4, of which waited for: 1 -> 1; matrix products, arithmetic and copies ran while one was open for 66% -> 71% of each run, Pallas kernels for 0% -> 0%
where the time goes in v1:
time: 409 us; the launch traced here: 406 us
  local copies, waits for them, and re-layouts  141 us (34%)
  matrix products  133 us (33%)
  blocking collectives  41.8 us (10%)
  other arithmetic  35.2 us (9%)
  waiting for transfers between devices  26.9 us (7%)
  starting transfers between devices  26.5 us (6%)
    dot_general x27, matrix products, near_step(): return total + jnp.dot(picked, operator, preferred_element_type=jnp.float32)  109 us
    gather x27, local copies, waits for them, and re-layouts, near_step(): picked = jnp.take(padded, rows, axis=0)  106 us
    all_gather x1, blocking collectives, _supply_ways(): local_out = jnp.sum(lax.all_gather(local_block, net_axis), axis=0)  41.8 us
    all_to_all x1, waiting for transfers between devices, local(): lax.all_to_all(send_velocity.reshape(devices, capacity, -1), 'leaf', spli...  26.9 us
    and x27, other arithmetic, near_step(): picked = jnp.take(padded, rows, axis=0)  21.3 us
    all_to_all x1, starting transfers between devices, local(): lax.all_to_all(send_alive.reshape(devices, capacity), 'leaf', split_axis=...  14 us
    dot_general x1, local copies, waits for them, and re-layouts, advect_rows(): jnp.dot(velocity_rows.reshape(-1, eval_ops.shape[0]), eval_ops[:, :nodes_...  10.8 us
  transfers between devices with their start and end apart: 4, of which 1 were waited for; matrix products, arithmetic and copies ran while one was open for 71% of the time, Pallas kernels for 0%

profile of v1, /device:TPU:1, one launch (start us, length us, event | category | flops | bytes accessed | tf_op | source)
XLA Modules:
  0.0 405.5 jit_solution(11100500127124011335)
XLA Ops:
  13.9 14.0 %all-to-all-start = ((bf16[128,1,16]{2,1,0:T(2,128)(2,1)}), bf16[128,1,16]{2,1,0:T(2,128)(2,1)S(1)}, u32[]{:S(2)}, u32[]{:S(2)}) async-start(bf16[128,1,16]{2,1,0:T(2,128)(2,1)} %all_to_all.12), calls=%async_computation | async-start | bytes 131072 | tf_op jit(solution)/shard_map/all_to_all | solution.py:139
  30.2 41.8 %all_gather.4 = f32[128,32,56]{2,1,0:T(8,128)} all-gather(f32[1,32,56]{2,1,0:T(8,128)S(1)} %broadcast_multiply_fusion), channel_id=1, replica_groups=mesh['leaf'=128] {'leaf'}, dimensions={0}, use_global_device_ids=true | all-gather | bytes 924672 | tf_op jit(solution)/shard_map/all_gather | solution.py:12
  76.0 7.5 %gather_fusion.1 = bf16[2048,220]{1,0:T(8,128)(2,1)S(1)} fusion(bf16[2048,220]{1,0:T(8,128)(2,1)S(1)} %copy.42, s32[2048]{0:T(1024)S(1)} %fusion.46), kind=kCustom, calls=%fused_computation.1 | custom fusion | bytes 1810432 | tf_op jit(solution)/shard_map/gather | solution.py:143
  87.6 237.2 %while.14 = (s32[]{:T(128)}, f32[1024,660]{0,1:T(8,128)}, s32[1024,27]{0,1:T(8,128)}, bf16[3072,220]{1,0:T(8,128)(2,1)S(1)}, bf16[27,220,660]{1,2,0:T(8,128)(2,1)}, /*index=5*/s32[]{:T(128)}, s32[]{:T(128)}) while((s32[]{:T(128)}, f32[1024,660]{0,1:T(8,128)}, s32[1024,27]{0,1:T(8,128)}, bf16[3072,220]{1,0:T(8,128)(2,1)S(1)}, ...), condition=%wide.region_1.2_spmd.clone, body=%wide.region_0.1_spmd.clone.sunk | while | flops 298953728 | bytes 7137383 | solution.py:89
  100.2 4.1 %select_add_fusion.2 = f32[1024,660]{0,1:T(8,128)} fusion(f32[1024,660]{0,1:T(8,128)} %get-tuple-element.192, pred[]{:T(512)S(6)} %compare.5, bf16[1024,220]{1,0:T(8,128)(2,1)S(1)} %gather_fusion, pred[1024]{0:T(1024)(128)(4,1)S(1)} %get-tuple-element.183, bf16[27,220,660]{1,2,0:T(8,128)(2,1)} %get-tuple-element.202, s32[]{:T(128)S(6)} %copy.93), kind=kOutput, calls=%fused_computation.2.clone.1 | convolution fusion | flops 298946560 | bytes 6214661 | tf_op jit(solution)/shard_map/while/body/eval_jaxpr/dot_general | solution.py:87
  109.1 4.1 %select_add_fusion.2 = f32[1024,660]{0,1:T(8,128)} fusion(f32[1024,660]{0,1:T(8,128)} %get-tuple-element.192, pred[]{:T(512)S(6)} %compare.5, bf16[1024,220]{1,0:T(8,128)(2,1)S(1)} %gather_fusion, pred[1024]{0:T(1024)(128)(4,1)S(1)} %get-tuple-element.183, bf16[27,220,660]{1,2,0:T(8,128)(2,1)} %get-tuple-element.202, s32[]{:T(128)S(6)} %copy.93), kind=kOutput, calls=%fused_computation.2.clone.1 | convolution fusion | flops 298946560 | bytes 6214661 | tf_op jit(solution)/shard_map/while/body/eval_jaxpr/dot_general | solution.py:87
  117.9 4.1 %select_add_fusion.2 = f32[1024,660]{0,1:T(8,128)} fusion(f32[1024,660]{0,1:T(8,128)} %get-tuple-element.192, pred[]{:T(512)S(6)} %compare.5, bf16[1024,220]{1,0:T(8,128)(2,1)S(1)} %gather_fusion, pred[1024]{0:T(1024)(128)(4,1)S(1)} %get-tuple-element.183, bf16[27,220,660]{1,2,0:T(8,128)(2,1)} %get-tuple-element.202, s32[]{:T(128)S(6)} %copy.93), kind=kOutput, calls=%fused_computation.2.clone.1 | convolution fusion | flops 298946560 | bytes 6214661 | tf_op jit(solution)/shard_map/while/body/eval_jaxpr/dot_general | solution.py:87
  126.7 4.1 %select_add_fusion.2 = f32[1024,660]{0,1:T(8,128)} fusion(f32[1024,660]{0,1:T(8,128)} %get-tuple-element.192, pred[]{:T(512)S(6)} %compare.5, bf16[1024,220]{1,0:T(8,128)(2,1)S(1)} %gather_fusion, pred[1024]{0:T(1024)(128)(4,1)S(1)} %get-tuple-element.183, bf16[27,220,660]{1,2,0:T(8,128)(2,1)} %get-tuple-element.202, s32[]{:T(128)S(6)} %copy.93), kind=kOutput, calls=%fused_computation.2.clone.1 | convolution fusion | flops 298946560 | bytes 6214661 | tf_op jit(solution)/shard_map/while/body/eval_jaxpr/dot_general | solution.py:87
  135.5 4.1 %select_add_fusion.2 = f32[1024,660]{0,1:T(8,128)} fusion(f32[1024,660]{0,1:T(8,128)} %get-tuple-element.192, pred[]{:T(512)S(6)} %compare.5, bf16[1024,220]{1,0:T(8,128)(2,1)S(1)} %gather_fusion, pred[1024]{0:T(1024)(128)(4,1)S(1)} %get-tuple-element.183, bf16[27,220,660]{1,2,0:T(8,128)(2,1)} %get-tuple-element.202, s32[]{:T(128)S(6)} %copy.93), kind=kOutput, calls=%fused_computation.2.clone.1 | convolution fusion | flops 298946560 | bytes 6214661 | tf_op jit(solution)/shard_map/while/body/eval_jaxpr/dot_general | solution.py:87
  153.2 4.1 %select_add_fusion.2 = f32[1024,660]{0,1:T(8,128)} fusion(f32[1024,660]{0,1:T(8,128)} %get-tuple-element.192, pred[]{:T(512)S(6)} %compare.5, bf16[1024,220]{1,0:T(8,128)(2,1)S(1)} %gather_fusion, pred[1024]{0:T(1024)(128)(4,1)S(1)} %get-tuple-element.183, bf16[27,220,660]{1,2,0:T(8,128)(2,1)} %get-tuple-element.202, s32[]{:T(128)S(6)} %copy.93), kind=kOutput, calls=%fused_computation.2.clone.1 | convolution fusion | flops 298946560 | bytes 6214661 | tf_op jit(solution)/shard_map/while/body/eval_jaxpr/dot_general | solution.py:87
  162.0 4.1 %select_add_fusion.2 = f32[1024,660]{0,1:T(8,128)} fusion(f32[1024,660]{0,1:T(8,128)} %get-tuple-element.192, pred[]{:T(512)S(6)} %compare.5, bf16[1024,220]{1,0:T(8,128)(2,1)S(1)} %gather_fusion, pred[1024]{0:T(1024)(128)(4,1)S(1)} %get-tuple-element.183, bf16[27,220,660]{1,2,0:T(8,128)(2,1)} %get-tuple-element.202, s32[]{:T(128)S(6)} %copy.93), kind=kOutput, calls=%fused_computation.2.clone.1 | convolution fusion | flops 298946560 | bytes 6214661 | tf_op jit(solution)/shard_map/while/body/eval_jaxpr/dot_general | solution.py:87
  170.8 4.1 %select_add_fusion.2 = f32[1024,660]{0,1:T(8,128)} fusion(f32[1024,660]{0,1:T(8,128)} %get-tuple-element.192, pred[]{:T(512)S(6)} %compare.5, bf16[1024,220]{1,0:T(8,128)(2,1)S(1)} %gather_fusion, pred[1024]{0:T(1024)(128)(4,1)S(1)} %get-tuple-element.183, bf16[27,220,660]{1,2,0:T(8,128)(2,1)} %get-tuple-element.202, s32[]{:T(128)S(6)} %copy.93), kind=kOutput, calls=%fused_computation.2.clone.1 | convolution fusion | flops 298946560 | bytes 6214661 | tf_op jit(solution)/shard_map/while/body/eval_jaxpr/dot_general | solution.py:87
  179.6 4.1 %select_add_fusion.2 = f32[1024,660]{0,1:T(8,128)} fusion(f32[1024,660]{0,1:T(8,128)} %get-tuple-element.192, pred[]{:T(512)S(6)} %compare.5, bf16[1024,220]{1,0:T(8,128)(2,1)S(1)} %gather_fusion, pred[1024]{0:T(1024)(128)(4,1)S(1)} %get-tuple-element.183, bf16[27,220,660]{1,2,0:T(8,128)(2,1)} %get-tuple-element.202, s32[]{:T(128)S(6)} %copy.93), kind=kOutput, calls=%fused_computation.2.clone.1 | convolution fusion | flops 298946560 | bytes 6214661 | tf_op jit(solution)/shard_map/while/body/eval_jaxpr/dot_general | solution.py:87
  188.4 4.1 %select_add_fusion.2 = f32[1024,660]{0,1:T(8,128)} fusion(f32[1024,660]{0,1:T(8,128)} %get-tuple-element.192, pred[]{:T(512)S(6)} %compare.5, bf16[1024,220]{1,0:T(8,128)(2,1)S(1)} %gather_fusion, pred[1024]{0:T(1024)(128)(4,1)S(1)} %get-tuple-element.183, bf16[27,220,660]{1,2,0:T(8,128)(2,1)} %get-tuple-element.202, s32[]{:T(128)S(6)} %copy.93), kind=kOutput, calls=%fused_computation.2.clone.1 | convolution fusion | flops 298946560 | bytes 6214661 | tf_op jit(solution)/shard_map/while/body/eval_jaxpr/dot_general | solution.py:87
  197.2 4.1 %select_add_fusion.2 = f32[1024,660]{0,1:T(8,128)} fusion(f32[1024,660]{0,1:T(8,128)} %get-tuple-element.192, pred[]{:T(512)S(6)} %compare.5, bf16[1024,220]{1,0:T(8,128)(2,1)S(1)} %gather_fusion, pred[1024]{0:T(1024)(128)(4,1)S(1)} %get-tuple-element.183, bf16[27,220,660]{1,2,0:T(8,128)(2,1)} %get-tuple-element.202, s32[]{:T(128)S(6)} %copy.93), kind=kOutput, calls=%fused_computation.2.clone.1 | convolution fusion | flops 298946560 | bytes 6214661 | tf_op jit(solution)/shard_map/while/body/eval_jaxpr/dot_general | solution.py:87
  206.1 4.1 %select_add_fusion.2 = f32[1024,660]{0,1:T(8,128)} fusion(f32[1024,660]{0,1:T(8,128)} %get-tuple-element.192, pred[]{:T(512)S(6)} %compare.5, bf16[1024,220]{1,0:T(8,128)(2,1)S(1)} %gather_fusion, pred[1024]{0:T(1024)(128)(4,1)S(1)} %get-tuple-element.183, bf16[27,220,660]{1,2,0:T(8,128)(2,1)} %get-tuple-element.202, s32[]{:T(128)S(6)} %copy.93), kind=kOutput, calls=%fused_computation.2.clone.1 | convolution fusion | flops 298946560 | bytes 6214661 | tf_op jit(solution)/shard_map/while/body/eval_jaxpr/dot_general | solution.py:87
  214.9 4.1 %select_add_fusion.2 = f32[1024,660]{0,1:T(8,128)} fusion(f32[1024,660]{0,1:T(8,128)} %get-tuple-element.192, pred[]{:T(512)S(6)} %compare.5, bf16[1024,220]{1,0:T(8,128)(2,1)S(1)} %gather_fusion, pred[1024]{0:T(1024)(128)(4,1)S(1)} %get-tuple-element.183, bf16[27,220,660]{1,2,0:T(8,128)(2,1)} %get-tuple-element.202, s32[]{:T(128)S(6)} %copy.93), kind=kOutput, calls=%fused_computation.2.clone.1 | convolution fusion | flops 298946560 | bytes 6214661 | tf_op jit(solution)/shard_map/while/body/eval_jaxpr/dot_general | solution.py:87
  232.5 4.1 %select_add_fusion.2 = f32[1024,660]{0,1:T(8,128)} fusion(f32[1024,660]{0,1:T(8,128)} %get-tuple-element.192, pred[]{:T(512)S(6)} %compare.5, bf16[1024,220]{1,0:T(8,128)(2,1)S(1)} %gather_fusion, pred[1024]{0:T(1024)(128)(4,1)S(1)} %get-tuple-element.183, bf16[27,220,660]{1,2,0:T(8,128)(2,1)} %get-tuple-element.202, s32[]{:T(128)S(6)} %copy.93), kind=kOutput, calls=%fused_computation.2.clone.1 | convolution fusion | flops 298946560 | bytes 6214661 | tf_op jit(solution)/shard_map/while/body/eval_jaxpr/dot_general | solution.py:87
  241.3 4.1 %select_add_fusion.2 = f32[1024,660]{0,1:T(8,128)} fusion(f32[1024,660]{0,1:T(8,128)} %get-tuple-element.192, pred[]{:T(512)S(6)} %compare.5, bf16[1024,220]{1,0:T(8,128)(2,1)S(1)} %gather_fusion, pred[1024]{0:T(1024)(128)(4,1)S(1)} %get-tuple-element.183, bf16[27,220,660]{1,2,0:T(8,128)(2,1)} %get-tuple-element.202, s32[]{:T(128)S(6)} %copy.93), kind=kOutput, calls=%fused_computation.2.clone.1 | convolution fusion | flops 298946560 | bytes 6214661 | tf_op jit(solution)/shard_map/while/body/eval_jaxpr/dot_general | solution.py:87
  259.0 4.1 %select_add_fusion.2 = f32[1024,660]{0,1:T(8,128)} fusion(f32[1024,660]{0,1:T(8,128)} %get-tuple-element.192, pred[]{:T(512)S(6)} %compare.5, bf16[1024,220]{1,0:T(8,128)(2,1)S(1)} %gather_fusion, pred[1024]{0:T(1024)(128)(4,1)S(1)} %get-tuple-element.183, bf16[27,220,660]{1,2,0:T(8,128)(2,1)} %get-tuple-element.202, s32[]{:T(128)S(6)} %copy.93), kind=kOutput, calls=%fused_computation.2.clone.1 | convolution fusion | flops 298946560 | bytes 6214661 | tf_op jit(solution)/shard_map/while/body/eval_jaxpr/dot_general | solution.py:87
  267.8 4.1 %select_add_fusion.2 = f32[1024,660]{0,1:T(8,128)} fusion(f32[1024,660]{0,1:T(8,128)} %get-tuple-element.192, pred[]{:T(512)S(6)} %compare.5, bf16[1024,220]{1,0:T(8,128)(2,1)S(1)} %gather_fusion, pred[1024]{0:T(1024)(128)(4,1)S(1)} %get-tuple-element.183, bf16[27,220,660]{1,2,0:T(8,128)(2,1)} %get-tuple-element.202, s32[]{:T(128)S(6)} %copy.93), kind=kOutput, calls=%fused_computation.2.clone.1 | convolution fusion | flops 298946560 | bytes 6214661 | tf_op jit(solution)/shard_map/while/body/eval_jaxpr/dot_general | solution.py:87
  285.4 4.1 %select_add_fusion.2 = f32[1024,660]{0,1:T(8,128)} fusion(f32[1024,660]{0,1:T(8,128)} %get-tuple-element.192, pred[]{:T(512)S(6)} %compare.5, bf16[1024,220]{1,0:T(8,128)(2,1)S(1)} %gather_fusion, pred[1024]{0:T(1024)(128)(4,1)S(1)} %get-tuple-element.183, bf16[27,220,660]{1,2,0:T(8,128)(2,1)} %get-tuple-element.202, s32[]{:T(128)S(6)} %copy.93), kind=kOutput, calls=%fused_computation.2.clone.1 | convolution fusion | flops 298946560 | bytes 6214661 | tf_op jit(solution)/shard_map/while/body/eval_jaxpr/dot_general | solution.py:87
  294.2 4.1 %select_add_fusion.2 = f32[1024,660]{0,1:T(8,128)} fusion(f32[1024,660]{0,1:T(8,128)} %get-tuple-element.192, pred[]{:T(512)S(6)} %compare.5, bf16[1024,220]{1,0:T(8,128)(2,1)S(1)} %gather_fusion, pred[1024]{0:T(1024)(128)(4,1)S(1)} %get-tuple-element.183, bf16[27,220,660]{1,2,0:T(8,128)(2,1)} %get-tuple-element.202, s32[]{:T(128)S(6)} %copy.93), kind=kOutput, calls=%fused_computation.2.clone.1 | convolution fusion | flops 298946560 | bytes 6214661 | tf_op jit(solution)/shard_map/while/body/eval_jaxpr/dot_general | solution.py:87
  311.9 4.1 %select_add_fusion.2 = f32[1024,660]{0,1:T(8,128)} fusion(f32[1024,660]{0,1:T(8,128)} %get-tuple-element.192, pred[]{:T(512)S(6)} %compare.5, bf16[1024,220]{1,0:T(8,128)(2,1)S(1)} %gather_fusion, pred[1024]{0:T(1024)(128)(4,1)S(1)} %get-tuple-element.183, bf16[27,220,660]{1,2,0:T(8,128)(2,1)} %get-tuple-element.202, s32[]{:T(128)S(6)} %copy.93), kind=kOutput, calls=%fused_computation.2.clone.1 | convolution fusion | flops 298946560 | bytes 6214661 | tf_op jit(solution)/shard_map/while/body/eval_jaxpr/dot_general | solution.py:87
  320.7 4.1 %select_add_fusion.2 = f32[1024,660]{0,1:T(8,128)} fusion(f32[1024,660]{0,1:T(8,128)} %get-tuple-element.192, pred[]{:T(512)S(6)} %compare.5, bf16[1024,220]{1,0:T(8,128)(2,1)S(1)} %gather_fusion, pred[1024]{0:T(1024)(128)(4,1)S(1)} %get-tuple-element.183, bf16[27,220,660]{1,2,0:T(8,128)(2,1)} %get-tuple-element.202, s32[]{:T(128)S(6)} %copy.93), kind=kOutput, calls=%fused_computation.2.clone.1 | convolution fusion | flops 298946560 | bytes 6214661 | tf_op jit(solution)/shard_map/while/body/eval_jaxpr/dot_general | solution.py:87
  330.4 4.5 %fusion.11 = bf16[2048,660]{0,1:T(8,128)(2,1)} fusion(bf16[1024,660]{1,0:T(8,128)(2,1)S(1)} %fusion.13, s32[1024]{0:T(1024)S(1)} %add_add_fusion), kind=kOutput, calls=%fused_computation.18 | convolution fusion | flops 2771689472 | bytes 4059136 | tf_op jit(solution)/shard_map/dot_general | solution.py:125
  334.9 4.6 %copy.51 = bf16[2048,660]{1,0:T(8,128)(2,1)} copy(bf16[2048,660]{0,1:T(8,128)(2,1)} %fusion.11) | data formatting | bytes 5406720 | tf_op jit(solution)/shard_map/convert_element_type | solution.py:125
  339.5 6.1 %all-to-all-start.1 = ((bf16[128,16,660]{2,1,0:T(8,128)(2,1)}), bf16[128,16,660]{2,1,0:T(8,128)(2,1)}, u32[]{:S(2)}, u32[]{:S(2)}) async-start(bf16[128,16,660]{2,1,0:T(8,128)(2,1)} %bitcast.102), calls=%async_computation.1 | async-start | bytes 6291456 | tf_op jit(solution)/shard_map/all_to_all | solution.py:132
  351.8 6.4 %fusion.28 = f32[2048,1024]{1,0:T(8,128)} fusion(bf16[220,1024]{1,0:T(8,128)(2,1)S(1)} %copy-done.4, bf16[2048,220]{0,1:T(8,128)(2,1)} %fusion.41, bf16[2048,220]{0,1:T(8,128)(2,1)} %fusion.19, bf16[2048,220]{1,0:T(8,128)(2,1)S(1)} %gather_fusion.1, pred[2048]{0:T(1024)(128)(4,1)S(1)} %get-tuple-element.144, pred[2048]{0:T(1024)(128)(4,1)S(1)} %get-tuple-element.139, ...), kind=kOutput, calls=%fused_computation.46 | convolution fusion | flops 1121894400 | bytes 11643424 | tf_op jit(solution)/shard_map/dot_general | solution.py:42
  360.0 26.9 %all-to-all-done.1 = bf16[128,16,660]{2,1,0:T(8,128)(2,1)} async-done(((bf16[128,16,660]{2,1,0:T(8,128)(2,1)}), bf16[128,16,660]{2,1,0:T(8,128)(2,1)}, u32[]{:S(2)}, u32[]{:S(2)}) %all-to-all-start.1) | async-done | bytes 2703392 | tf_op jit(solution)/shard_map/all_to_all | solution.py:132
  386.9 10.8 %dot_general.78 = bf16[2048,3,220]{2,1,0:T(4,128)(2,1)} reshape(bf16[128,16,660]{2,1,0:T(8,128)(2,1)} %all-to-all-done.1) | data formatting | bytes 5406720 | tf_op jit(solution)/shard_map/dot_general | solution.py:44
  400.9 4.6 %fusion.26 = bf16[2048,256]{1,0:T(8,128)(2,1)} fusion(f32[2048,1024]{1,0:T(8,128)} %fusion.28, f32[2048,3,256]{2,0,1:T(8,128)S(1)} %fusion.14, f32[2048]{0:T(1024)S(1)} %reshape.132), kind=kLoop, calls=%fused_computation.38 | loop fusion | flops 4718592 | bytes 15736832 | tf_op jit(solution)/shard_map/convert_element_type | solution.py:53
  (172 shorter events, 191.3 us)
Async XLA Ops:
  0.6 74.4 %copy-start = (bf16[8,56,220]{2,1,0:T(8,128)(2,1)S(1)}, bf16[8,56,220]{2,1,0:T(8,128)(2,1)}, u32[]{:S(2)}) copy-start(bf16[8,56,220]{2,1,0:T(8,128)(2,1)} %param.23) | copy-start | bytes 591364
  0.6 10.6 %copy-start.14 = (s32[1024,1]{0,1:T(1,128)S(1)}, s32[1024,1]{0,1:T(1,128)}, u32[]{:S(2)}) copy-start(s32[1024,1]{0,1:T(1,128)} %param.24) | copy-start | bytes 12292
  3.6 82.3 %collective-permute-start.1 = (bf16[1024,220]{1,0:T(8,128)(2,1)}, bf16[1024,220]{1,0:T(8,128)(2,1)}, u32[]{:S(2)}, u32[]{:S(2)}) collective-permute-start(bf16[1024,220]{1,0:T(8,128)(2,1)} %multiply_convert_fusion), channel_id=1, source_target_pairs={{1,0},{2,1},{3,2},{4,3},{5,4},{6,5},{7,6},{8,7},{9,8},{10,9},{11,1... | collective-permute-start | bytes 1351688 | tf_op jit(solution)/shard_map/ppermute | solution.py:27
  6.9 79.0 %collective-permute-start = (bf16[1024,220]{1,0:T(8,128)(2,1)}, bf16[1024,220]{1,0:T(8,128)(2,1)}, u32[]{:S(2)}, u32[]{:S(2)}) collective-permute-start(bf16[1024,220]{1,0:T(8,128)(2,1)} %multiply_convert_fusion), channel_id=1, source_target_pairs={{0,1},{1,2},{2,3},{3,4},{4,5},{5,6},{6,7},{7,8},{8,9},{9,10},{10,1... | collective-permute-start | bytes 1351688 | tf_op jit(solution)/shard_map/ppermute | solution.py:24
  11.3 16.9 %copy-start.16 = (s32[2048]{0:T(1024)S(1)}, s32[2048]{0:T(1024)}, u32[]{:S(2)}) copy-start(s32[2048]{0:T(1024)} %param.26) | copy-start | bytes 24580
  11.3 16.9 %copy-start.15 = (s32[2048]{0:T(1024)S(1)}, s32[2048]{0:T(1024)}, u32[]{:S(2)}) copy-start(s32[2048]{0:T(1024)} %param.27) | copy-start | bytes 24580
  11.3 16.9 %copy-start.3 = (bf16[2048,220]{0,1:T(8,128)(2,1)S(1)}, bf16[2048,220]{0,1:T(8,128)(2,1)}, u32[]{:S(2)}) copy-start(bf16[2048,220]{0,1:T(8,128)(2,1)} %param.25) | copy-start | bytes 2703364
  13.9 325.6 %all-to-all-start = ((bf16[128,1,16]{2,1,0:T(2,128)(2,1)}), bf16[128,1,16]{2,1,0:T(2,128)(2,1)S(1)}, u32[]{:S(2)}, u32[]{:S(2)}) async-start(bf16[128,1,16]{2,1,0:T(2,128)(2,1)} %all_to_all.12), calls=%async_computation | async-start | bytes 131072 | tf_op jit(solution)/shard_map/all_to_all | solution.py:139
  28.8 45.1 %copy-start.13 = (f32[56,168]{1,0:T(8,128)S(1)}, f32[56,168]{1,0:T(8,128)}, u32[]{:S(2)}) copy-start(f32[56,168]{1,0:T(8,128)} %param.21) | copy-start | bytes 112900
  28.8 46.5 %copy-start.12 = (s32[1024,27]{0,1:T(8,128)S(1)}, s32[1024,27]{0,1:T(8,128)}, u32[]{:S(2)}) copy-start(s32[1024,27]{0,1:T(8,128)} %param.18) | copy-start | bytes 331780
  76.0 7.5 %copy-start.2 = (bf16[8,220,220]{2,0,1:T(8,128)(2,1)S(1)}, bf16[8,220,220]{2,0,1:T(8,128)(2,1)}, u32[]{:S(2)}) copy-start(bf16[8,220,220]{2,0,1:T(8,128)(2,1)} %param.28) | copy-start | bytes 2323204
  339.5 6.1 %copy-start.9 = (bf16[1,220,220]{2,0,1:T(2,128)(2,1)S(1)}, bf16[1,220,220]{2,0,1:T(2,128)(2,1)}, u32[]{:S(2)}) copy-start(bf16[1,220,220]{2,0,1:T(2,128)(2,1)} %get-tuple-element.132) | copy-start | bytes 290404
  339.5 6.6 %copy-start.8 = (bf16[1,220,220]{2,0,1:T(2,128)(2,1)S(1)}, bf16[1,220,220]{2,0,1:T(2,128)(2,1)}, u32[]{:S(2)}) copy-start(bf16[1,220,220]{2,0,1:T(2,128)(2,1)} %get-tuple-element.133) | copy-start | bytes 290404
  339.5 47.4 %all-to-all-start.1 = ((bf16[128,16,660]{2,1,0:T(8,128)(2,1)}), bf16[128,16,660]{2,1,0:T(8,128)(2,1)}, u32[]{:S(2)}, u32[]{:S(2)}) async-start(bf16[128,16,660]{2,1,0:T(8,128)(2,1)} %bitcast.102), calls=%async_computation.1 | async-start | bytes 6291456 | tf_op jit(solution)/shard_map/all_to_all | solution.py:132
  345.6 1.1 copy-start.7
  345.6 1.6 copy-start.6
  346.1 1.6 copy-start.5
  346.7 2.5 copy-start.11
  349.2 0.9 copy-start.10
  349.9 2.0 copy-start.4
  400.9 4.6 %copy-start.1 = (bf16[8,56,220]{2,1,0:T(8,128)(2,1)S(1)}, bf16[8,56,220]{2,1,0:T(8,128)(2,1)}, u32[]{:S(2)}) copy-start(bf16[8,56,220]{2,1,0:T(8,128)(2,1)} %param.23) | copy-start | bytes 591364
